TPU v7x, 32 devices: a whole 2x2x4 slice. The times are simulated.
32 devices in a mesh: groups: 2 (over x), seq: 8 (over z, y), chan: 2 (over core).
Axes of the slice: x: 2, y: 2, z: 4, core: 2. Of those that a mesh axis runs over, the one named last changes fastest.
Arguments:
- inputs: bfloat16 [8192, 768], P(('groups', 'seq')), parts along dimension 0, may hold values from -6 to 6
- enc_weight: bfloat16 [768, 5, 1536], P('seq', None, 'chan'), may hold values from -0.09375 to 0.09375
- dec_weight: bfloat16 [768, 5, 1536], P('seq', None, 'chan'), may hold values from -0.0625 to 0.0625
- cotangent: bfloat16 [8192, 768], P(('groups', 'seq'), 'chan'), parts along dimension 0, may hold values from -6 to 6
Outputs:
- mixed_out: bfloat16 [8192, 768], P(('groups', 'seq'), 'chan'), parts along dimension 0
- input_grad: bfloat16 [8192, 768], P(('groups', 'seq'), 'chan'), parts along dimension 0
- enc_grad: bfloat16 [1536, 5, 1536], P(('groups', 'seq'), None, 'chan'), parts along dimension 0
- dec_grad: bfloat16 [1536, 5, 1536], P(('groups', 'seq'), None, 'chan'), parts along dimension 0
There are 2 independent parts, one for each index of `groups`. A program takes and returns all parts, laid end to end along the dimension named above; an argument that names none is the same for every part. Nothing has to cross between parts.
All inputs are finite; a program needn't handle non-finite values.
Results may differ from a plain program's by a relative error of at most 0.012.
Values may be sent and summed in bfloat16 or wider, within the bound.
A program may use at most 128 MiB of HBM per device.

v0:
```python
import jax
import jax.numpy as jnp
from jax import lax
from jax.sharding import PartitionSpec as P


def with_halo(array, sides, width):
    for axis, dim in sides:
        size, length = (lax.axis_size(axis), array.shape[dim])
        up = [(i, (i + 1) % size) for i in range(size - 1)]
        down = [(j, i) for i, j in up]
        last = lax.slice_in_dim(array, length - width, length, axis=dim)
        first = lax.slice_in_dim(array, 0, width, axis=dim)
        before = lax.ppermute(last, axis, up)
        after = lax.ppermute(first, axis, down)
        array = jnp.concatenate([before, array, after], axis=dim)
    return array


def gelu_fn(values):
    return jax.nn.gelu(values, approximate=True)


def shards(inputs, enc_weight, dec_weight, cotangent):
    row_count = inputs.shape[0]
    half_rows = row_count // 2
    fine_width = inputs.shape[1]
    share_width = cotangent.shape[1]
    taps = enc_weight.shape[1]
    coarse_share = enc_weight.shape[2]
    contract_last = (((1,), (1,)), ((), ()))
    enc_full = lax.all_gather(enc_weight, "seq", axis=0, tiled=True)
    dec_full = lax.all_gather(dec_weight, "seq", axis=0, tiled=True)
    pooled = (
        inputs.astype(jnp.float32).reshape(half_rows, 2, fine_width).sum(axis=1) * 0.5
    ).astype(jnp.bfloat16)
    pad_pool = with_halo(pooled, (("seq", 0),), 2)
    pre_act = jnp.zeros((half_rows, coarse_share), jnp.float32)
    for tap_index in range(taps):
        pre_act = pre_act + jnp.dot(
            pad_pool[tap_index : tap_index + half_rows],
            enc_full[:, tap_index, :],
            preferred_element_type=jnp.float32,
        )
    hidden = gelu_fn(pre_act).astype(jnp.bfloat16)
    pad_hidden = with_halo(hidden, (("seq", 0),), 1)
    pad_up = jnp.repeat(pad_hidden, 2, axis=0)
    dec_part = jnp.zeros((row_count, fine_width), jnp.float32)
    for tap_index in range(taps):
        dec_part = dec_part + lax.dot_general(
            pad_up[tap_index : tap_index + row_count],
            dec_full[:, tap_index, :],
            contract_last,
            preferred_element_type=jnp.float32,
        )
    dec_share = lax.psum_scatter(
        dec_part.astype(jnp.bfloat16), "chan", scatter_dimension=1, tiled=True
    ).astype(jnp.float32)
    col_start = lax.axis_index("chan") * share_width
    skip_cols = lax.dynamic_slice_in_dim(inputs, col_start, share_width, 1)
    mixed_out = (skip_cols.astype(jnp.float32) + dec_share).astype(jnp.bfloat16)
    cot_full = lax.all_gather(cotangent, "chan", axis=1, tiled=True)
    pad_cot = with_halo(cot_full, (("seq", 0),), 2)
    up_grad = jnp.zeros((row_count, coarse_share), jnp.float32)
    for tap_index in range(taps):
        up_grad = up_grad + jnp.dot(
            pad_cot[4 - tap_index : 4 - tap_index + row_count],
            dec_full[:, tap_index, :],
            preferred_element_type=jnp.float32,
        )
    hid_grad = up_grad.reshape(half_rows, 2, coarse_share).sum(axis=1)
    _, pullback = jax.vjp(gelu_fn, pre_act)
    pre_grad = pullback(hid_grad)[0].astype(jnp.bfloat16)
    pad_grad = with_halo(pre_grad, (("seq", 0),), 2)
    pool_grad = jnp.zeros((half_rows, fine_width), jnp.float32)
    for tap_index in range(taps):
        pool_grad = pool_grad + lax.dot_general(
            pad_grad[4 - tap_index : 4 - tap_index + half_rows],
            enc_full[:, tap_index, :],
            contract_last,
            preferred_element_type=jnp.float32,
        )
    total_sum = lax.psum(pool_grad.astype(jnp.bfloat16), "chan").astype(jnp.float32)
    grad_share = lax.dynamic_slice_in_dim(total_sum, col_start, share_width, 1)
    input_grad = (cotangent.astype(jnp.float32) + 0.5 * jnp.repeat(grad_share, 2, axis=0)).astype(
        jnp.bfloat16
    )

    def dec_terms():
        return jnp.stack(
            [
                jnp.dot(
                    cot_full.T,
                    pad_up[tap_index : tap_index + row_count],
                    preferred_element_type=jnp.float32,
                )
                for tap_index in range(taps)
            ],
            axis=1,
        )

    joint_sum = lax.psum_scatter(
        jnp.concatenate(
            [
                jnp.stack(
                    [
                        jnp.dot(
                            pad_pool[tap_index : tap_index + half_rows].T,
                            pre_grad,
                            preferred_element_type=jnp.float32,
                        )
                        for tap_index in range(taps)
                    ],
                    axis=1,
                ),
                dec_terms(),
            ],
            axis=2,
        ).astype(jnp.bfloat16),
        "seq",
        scatter_dimension=0,
        tiled=True,
    ).astype(jnp.float32)
    enc_sum = joint_sum[:, :, :coarse_share]
    dec_sum = joint_sum[:, :, coarse_share:]
    return (mixed_out, input_grad, enc_sum.astype(jnp.bfloat16), dec_sum.astype(jnp.bfloat16))


def solution(mesh):
    return jax.shard_map(
        shards,
        mesh=mesh,
        in_specs=(
            P(("groups", "seq"), None),
            P("seq", None, "chan"),
            P("seq", None, "chan"),
            P(("groups", "seq"), "chan"),
        ),
        out_specs=(
            P(("groups", "seq"), "chan"),
            P(("groups", "seq"), "chan"),
            P(("groups", "seq"), None, "chan"),
            P(("groups", "seq"), None, "chan"),
        ),
        check_vma=False,
    )
```

profile of v0, /device:TPU:0, one launch (start us, length us, event | category | flops | bytes accessed | tf_op | source)
XLA Modules:
  0.0 509.0 jit_solution(5221697619440300852)
XLA Ops:
  7.2 0.7 all-gather.5.cloned.1.call-update
  8.0 0.7 all-gather.3.cloned.1.call-update
  8.7 2.7 all_gather.11
  11.4 1.3 collective-permute-start.4
  12.7 5.4 %collective-permute-start.5 = (bf16[2,768]{1,0:T(2,128)(2,1)S(1)}, bf16[2,768]{1,0:T(2,128)(2,1)S(1)}, u32[]{:S(2)}, u32[]{:S(2)}) collective-permute-start(bf16[2,768]{1,0:T(2,128)(2,1)S(1)} %get-tuple-element.17), channel_id=1, source_target_pairs={{0,2},{2,4},{4,6},{6,8},{8,10},{10,12},{12,14},{1,3},{3,5},{5,7},{... | collective-permute-start | bytes 9224 | tf_op jit(solution)/shard_map/ppermute | solution.py:14
  18.1 0.8 reshape.31
  18.9 1.9 reduce_sum.18
  20.8 4.8 collective-permute-start
  25.7 1.5 collective-permute-start.1
  27.2 80.0 %all-gather.5.cloned.1.call-done = bf16[768,5,768]{2,0,1:T(8,128)(2,1)} async-done(((bf16[96,5,768]{2,0,1:T(8,128)(2,1)}), bf16[768,5,768]{2,0,1:T(8,128)(2,1)}) %all-gather.5.cloned.1.call-update) | async-done | bytes 5898256 | tf_op jit(solution)/shard_map/all_gather | solution.py:33
  107.2 2.2 fusion.37
  109.4 2.1 fusion.33
  111.5 0.8 fusion.31
  112.3 0.8 fusion.35
  113.1 2.1 add_add_fusion
  115.2 86.7 %all-gather.3.cloned.1.call-done = bf16[768,5,768]{2,0,1:T(8,128)(2,1)} async-done(((bf16[96,5,768]{2,0,1:T(8,128)(2,1)}), bf16[768,5,768]{2,0,1:T(8,128)(2,1)}) %all-gather.3.cloned.1.call-update) | async-done | bytes 5898256 | tf_op jit(solution)/shard_map/all_gather | solution.py:32
  201.9 1.7 fusion.28
  203.6 2.6 fusion.30
  206.3 2.2 reshape.29
  208.5 2.9 reduce_sum.19
  211.4 1.8 fusion.26
  213.2 1.9 fusion.23
  215.1 2.2 fusion.48
  217.3 0.6 fusion.81
  217.9 0.6 fusion.80
  218.5 1.3 collective-permute-start.6
  219.8 4.5 collective-permute-start.7
  224.4 3.4 collective-permute-start.2
  227.7 1.5 collective-permute-start.3
  230.0 0.5 fusion.11
  230.5 0.5 fusion.13
  231.0 0.5 fusion.15
  231.5 2.7 fusion.27
  234.2 3.2 fusion.36
  237.9 0.5 fusion.19
  238.5 2.5 copy-done
  241.5 1.2 reshape.28
  244.0 1.2 slice.169
  245.2 2.4 fusion.38
  247.7 2.2 fusion.34
  249.9 2.2 fusion.32
  252.2 2.3 add_convert_fusion
  254.5 1.9 fusion.1
  256.4 0.5 fusion.29
  256.9 1.3 fusion.25
  258.2 1.2 fusion.21
  259.4 1.3 fusion.24
  261.1 3.1 fusion.3
  264.1 1.2 copy.12
  265.3 1.9 fusion.5
  267.3 1.8 fusion.7
  269.1 1.9 fusion.9
  271.0 10.2 %pad_maximum_fusion = bf16[768,5,1536]{0,2,1:T(8,128)(2,1)} fusion(bf16[768,5,768]{0,2,1:T(8,128)(2,1)} %fusion.9, bf16[768,5,768]{0,2,1:T(8,128)(2,1)} %copy-done), kind=kLoop, calls=%fused_computation | loop fusion | flops 23592960 | bytes 23592960 | tf_op jit(solution)/shard_map/concatenate | solution.py:103
  281.2 16.4 %copy.16 = bf16[768,7680]{1,0:T(8,128)(2,1)} copy(bf16[768,7680]{0,1:T(8,128)(2,1)} %bitcast.119) | data formatting | bytes 23592960
  297.7 1.0 convert_multiply_fusion
  299.0 0.5 mul.82
  299.6 0.8 add_convert_fusion.1
  300.4 1.2 copy.13
  301.6 0.8 add_convert_fusion.2
  302.5 192.3 %reduce-scatter.9.cloned.1.call-done = bf16[96,7680]{1,0:T(8,128)(2,1)} async-done(((bf16[768,7680]{1,0:T(8,128)(2,1)}), bf16[96,7680]{1,0:T(8,128)(2,1)}) %reduce-scatter.9.cloned.1.call-update) | async-done | bytes 1474576
  494.8 2.7 copy.17
  497.5 1.5 fusion.78
  499.0 2.3 copy.11
  501.2 1.2 copy.10
  (71 shorter events, 4.0 us)
Async XLA Ops:
  7.2 10.9 %copy-start.3 = (bf16[512,768]{1,0:T(8,128)(2,1)S(1)}, bf16[512,768]{1,0:T(8,128)(2,1)}, u32[]{:S(2)}) copy-start(bf16[512,768]{1,0:T(8,128)(2,1)} %param.4) | copy-start | bytes 2359300
  7.2 100.0 %all-gather.5.cloned.1.call-start = ((), (), s32[]{:S(2)}) async-start(), calls=%async_computation.3 | async-start | bytes 6635520 | tf_op jit(solution)/shard_map/all_gather | solution.py:33
  7.9 194.0 %all-gather.3.cloned.1.call-start = ((), (), s32[]{:S(2)}) async-start(), calls=%async_computation.2 | async-start | bytes 6635520 | tf_op jit(solution)/shard_map/all_gather | solution.py:32
  8.7 289.0 %all-reduce.2.cloned.1.call-start = ((), (), s32[]{:S(2)}) async-start(), calls=%async_computation.4 | async-start | bytes 786432 | tf_op jit(solution)/shard_map/psum | solution.py:83
  11.4 15.8 %collective-permute-start.4 = (bf16[2,768]{1,0:T(2,128)(2,1)S(1)}, bf16[2,768]{1,0:T(2,128)(2,1)S(1)}, u32[]{:S(2)}, u32[]{:S(2)}) collective-permute-start(bf16[2,768]{1,0:T(2,128)(2,1)S(1)} %get-tuple-element.16), channel_id=1, source_target_pairs={{2,0},{4,2},{6,4},{8,6},{10,8},{12,10},{14,12},{3,1},{5,3},{7,5},{... | collective-permute-start | bytes 9224 | tf_op jit(solution)/shard_map/ppermute | solution.py:15
  12.7 14.6 %collective-permute-start.5 = (bf16[2,768]{1,0:T(2,128)(2,1)S(1)}, bf16[2,768]{1,0:T(2,128)(2,1)S(1)}, u32[]{:S(2)}, u32[]{:S(2)}) collective-permute-start(bf16[2,768]{1,0:T(2,128)(2,1)S(1)} %get-tuple-element.17), channel_id=1, source_target_pairs={{0,2},{2,4},{4,6},{6,8},{8,10},{10,12},{12,14},{1,3},{3,5},{5,7},{... | collective-permute-start | bytes 9224 | tf_op jit(solution)/shard_map/ppermute | solution.py:14
  20.8 190.6 %collective-permute-start = (bf16[2,768]{1,0:T(2,128)(2,1)S(1)}, bf16[2,768]{1,0:T(2,128)(2,1)S(1)}, u32[]{:S(2)}, u32[]{:S(2)}) collective-permute-start(bf16[2,768]{1,0:T(2,128)(2,1)S(1)} %get-tuple-element.24), channel_id=1, source_target_pairs={{0,2},{2,4},{4,6},{6,8},{8,10},{10,12},{12,14},{1,3},{3,5},{5,7},{... | collective-permute-start | bytes 9224 | tf_op jit(solution)/shard_map/ppermute | solution.py:14
  25.7 178.0 %collective-permute-start.1 = (bf16[2,768]{1,0:T(2,128)(2,1)S(1)}, bf16[2,768]{1,0:T(2,128)(2,1)S(1)}, u32[]{:S(2)}, u32[]{:S(2)}) collective-permute-start(bf16[2,768]{1,0:T(2,128)(2,1)S(1)} %get-tuple-element.25), channel_id=1, source_target_pairs={{2,0},{4,2},{6,4},{8,6},{10,8},{12,10},{14,12},{3,1},{5,3},{7,5},{... | collective-permute-start | bytes 9224 | tf_op jit(solution)/shard_map/ppermute | solution.py:15
  107.2 4.3 copy-start.7
  203.6 11.5 %copy-start.14 = (bf16[2,768]{1,0:T(2,128)(2,1)}, bf16[2,768]{1,0:T(2,128)(2,1)S(1)}, u32[]{:S(2)}) copy-start(bf16[2,768]{1,0:T(2,128)(2,1)S(1)} %collective-permute-done.1) | copy-start | bytes 9220
  213.2 1.9 copy-start.10
  213.2 1.9 copy-start.16
  218.5 38.4 %collective-permute-start.6 = (bf16[2,768]{1,0:T(2,128)(2,1)}, bf16[2,768]{1,0:T(2,128)(2,1)}, u32[]{:S(2)}, u32[]{:S(2)}) collective-permute-start(bf16[2,768]{1,0:T(2,128)(2,1)} %get-tuple-element.18), channel_id=1, source_target_pairs={{2,0},{4,2},{6,4},{8,6},{10,8},{12,10},{14,12},{3,1},{5,3},{7,5},{... | collective-permute-start | bytes 9224 | tf_op jit(solution)/shard_map/ppermute | solution.py:15
  219.8 36.6 %collective-permute-start.7 = (bf16[2,768]{1,0:T(2,128)(2,1)}, bf16[2,768]{1,0:T(2,128)(2,1)S(1)}, u32[]{:S(2)}, u32[]{:S(2)}) collective-permute-start(bf16[2,768]{1,0:T(2,128)(2,1)} %get-tuple-element.19), channel_id=1, source_target_pairs={{0,2},{2,4},{4,6},{6,8},{8,10},{10,12},{12,14},{1,3},{3,5},{5,7},{... | collective-permute-start | bytes 9224 | tf_op jit(solution)/shard_map/ppermute | solution.py:14
  224.4 16.6 %collective-permute-start.2 = (bf16[1,768]{1,0:T(2,128)(2,1)}, bf16[1,768]{1,0:T(2,128)(2,1)S(1)}, u32[]{:S(2)}, u32[]{:S(2)}) collective-permute-start(bf16[1,768]{1,0:T(2,128)(2,1)} %get-tuple-element.22), channel_id=1, source_target_pairs={{0,2},{2,4},{4,6},{6,8},{8,10},{10,12},{12,14},{1,3},{3,5},{5,7},{... | collective-permute-start | bytes 4616 | tf_op jit(solution)/shard_map/ppermute | solution.py:14
  227.7 13.3 %collective-permute-start.3 = (bf16[1,768]{1,0:T(2,128)(2,1)}, bf16[1,768]{1,0:T(2,128)(2,1)S(1)}, u32[]{:S(2)}, u32[]{:S(2)}) collective-permute-start(bf16[1,768]{1,0:T(2,128)(2,1)} %get-tuple-element.23), channel_id=1, source_target_pairs={{2,0},{4,2},{6,4},{8,6},{10,8},{12,10},{14,12},{3,1},{5,3},{7,5},{... | collective-permute-start | bytes 4616 | tf_op jit(solution)/shard_map/ppermute | solution.py:15
  230.0 4.2 copy-start.11
  234.2 3.2 copy-start.15
  238.5 2.5 copy-start
  245.2 2.4 copy-start.8
  247.7 2.3 copy-start.13
  247.7 4.5 copy-start.6
  249.9 6.4 %slice-start = ((s8[5898240]{0:T(1024)(128)(4,1)}), s8[4194304]{0:T(1024)(128)(4,1)S(1)}, s32[]{:S(2)}) async-start(s8[5898240]{0:T(1024)(128)(4,1)} %bitcast.121), calls=%async_computation.7 | async-start | bytes 8388608
  252.2 4.2 slice-start.1
  256.9 1.3 copy-start.2
  260.8 4.6 copy-start.12
  260.8 39.6 %reduce-scatter.7.cloned.1.call-start = ((), (), s32[]{:S(2)}) async-start(), calls=%async_computation.5 | async-start | bytes 1179648
  265.3 1.9 copy-start.9
  267.2 227.6 %reduce-scatter.9.cloned.1.call-start = ((), (), s32[]{:S(2)}) async-start(), calls=%async_computation.6 | async-start | bytes 13271040
  297.7 1.9 copy-start.5
  299.0 2.6 copy-start.4
  499.0 2.3 copy-start.1
Sparse Core Ops, SparseCore 0:
  10.2 96.9 all-gather.4
  109.4 92.4 all-gather.2
  260.9 19.2 all-reduce.1
  282.3 9.3 reduce-scatter.6
  297.8 196.9 reduce-scatter.8
where the time goes:
time: 510 us; the launch traced here: 509 us
  waiting for transfers between devices  360 us (71%)
  matrix products  50.6 us (10%)
  local copies, waits for them, and re-layouts  38.8 us (8%)
  starting transfers between devices  24.2 us (5%)
  other arithmetic  18 us (4%)
  between operations  14.4 us (3%)
    unnamed x7, waiting for transfers between devices  194 us
    all_gather x1, waiting for transfers between devices, shards(): enc_full = lax.all_gather(enc_weight, 'seq', axis=0, tiled=True)  86.7 us
    all_gather x1, waiting for transfers between devices, shards(): dec_full = lax.all_gather(dec_weight, 'seq', axis=0, tiled=True)  80 us
    unnamed x45, local copies, waits for them, and re-layouts  27.7 us
    ppermute x4, starting transfers between devices, with_halo(): before = lax.ppermute(last, axis, up)  18.1 us
    dot_general x5, matrix products, shards(): lax.dot_general(pad_up[tap_index:tap_index + row_count], dec_full[:, tap_...  12.4 us
    dot_general x5, matrix products, dec_terms(): jnp.dot(cot_full.T, pad_up[tap_index:tap_index + row_count], preferred_el...  10.5 us
    dot_general x5, matrix products, shards(): jnp.dot(pad_pool[tap_index:tap_index + half_rows], enc_full[:, tap_index,...  10.2 us
  transfers between devices with their start and end apart: 13, of which 3 were waited for; matrix products, arithmetic and copies ran while one was open for 17% of the time, Pallas kernels for 0%

commit v1 on v0

--- a/solution.py
+++ b/solution.py
@@ -2,6 +2,18 @@
 import jax.numpy as jnp
 from jax import lax
 from jax.sharding import PartitionSpec as P
+
+
+def collect(array, axis, dim):
+    ways, here, hop = (lax.axis_size(axis), lax.axis_index(axis), array.shape[dim])
+    dims = [n * ways if d == dim else n for d, n in enumerate(array.shape)]
+    full = lax.dynamic_update_slice_in_dim(
+        jnp.zeros(dims, array.dtype), array, here * hop, axis=dim
+    )
+    for far in range(1, ways):
+        array = lax.ppermute(array, axis, [(d, (d + 1) % ways) for d in range(ways)])
+        full = lax.dynamic_update_slice_in_dim(full, array, (here - far) % ways * hop, axis=dim)
+    return full
 
 
 def with_halo(array, sides, width):
@@ -30,7 +42,7 @@
     coarse_share = enc_weight.shape[2]
     contract_last = (((1,), (1,)), ((), ()))
     enc_full = lax.all_gather(enc_weight, "seq", axis=0, tiled=True)
-    dec_full = lax.all_gather(dec_weight, "seq", axis=0, tiled=True)
+    dec_full = collect(dec_weight, "seq", 0)
     pooled = (
         inputs.astype(jnp.float32).reshape(half_rows, 2, fine_width).sum(axis=1) * 0.5
     ).astype(jnp.bfloat16)

time: 510 us -> 537 us (1.053)
  matrix products: 50.6 us -> 66.3 us
  local copies, waits for them, and re-layouts: 38.8 us -> 53.5 us
    ppermute x0 -> x7, waiting for transfers between devices: none -> 164 us  [collect(): lax.ppermute(array, axis, [(d, (d + 1) % ways) for d in range(ways)])]
    all_gather x1, waiting for transfers between devices: 86.7 us -> 0.02 us  [shards(): enc_full = lax.all_gather(enc_weight, 'seq', axis=0, tiled=True)]
    all_gather x1 -> x0, waiting for transfers between devices: 80 us -> none  [shards(): dec_full = lax.all_gather(dec_weight, 'seq', axis=0, tiled=True)]
    dynamic_update_slice x0 -> x8, local copies, waits for them, and re-layouts: none -> 12 us  [the longest x7 11 us: collect(): lax.dynamic_update_slice_in_dim(full, array, (here - far) % ways * hop, a...]
    ppermute x4, starting transfers between devices: 18.1 us -> 12.3 us  [with_halo(): before = lax.ppermute(last, axis, up)]
    dot_general x5, matrix products: 12.4 us -> 18.1 us  [shards(): lax.dot_general(pad_up[tap_index:tap_index + row_count], dec_full[:, tap_...]
    unnamed x7 -> x6, waiting for transfers between devices: 194 us -> 196 us
    unnamed x45 -> x33, local copies, waits for them, and re-layouts: 27.7 us -> 26.2 us
  transfers between devices with their start and end apart: 13 -> 19, of which waited for: 3 -> 8; matrix products, arithmetic and copies ran while one was open for 17% -> 21% of each run, Pallas kernels for 0% -> 0%
where the time goes in v1:
time: 537 us; the launch traced here: 535 us
  waiting for transfers between devices  359 us (67%)
  matrix products  66.3 us (12%)
  local copies, waits for them, and re-layouts  53.5 us (10%)
  starting transfers between devices  21.6 us (4%)
  other arithmetic  17.1 us (3%)
  between operations  14.5 us (3%)
    unnamed x6, waiting for transfers between devices  196 us
    ppermute x7, waiting for transfers between devices, collect(): lax.ppermute(array, axis, [(d, (d + 1) % ways) for d in range(ways)])  164 us
    unnamed x33, local copies, waits for them, and re-layouts  26.2 us
    dot_general x5, matrix products, shards(): lax.dot_general(pad_up[tap_index:tap_index + row_count], dec_full[:, tap_...  18.1 us
    dot_general x5, matrix products, dec_terms(): jnp.dot(cot_full.T, pad_up[tap_index:tap_index + row_count], preferred_el...  12.8 us
    ppermute x4, starting transfers between devices, with_halo(): before = lax.ppermute(last, axis, up)  12.3 us
    dot_general x5, matrix products, shards(): jnp.dot(pad_cot[4 - tap_index:4 - tap_index + row_count], dec_full[:, tap...  11.6 us
    dynamic_update_slice x7, local copies, waits for them, and re-layouts, collect(): lax.dynamic_update_slice_in_dim(full, array, (here - far) % ways * hop, a...  11 us
  transfers between devices with their start and end apart: 19, of which 8 were waited for; matrix products, arithmetic and copies ran while one was open for 21% of the time, Pallas kernels for 0%

profile of v1, /device:TPU:0, one launch (start us, length us, event | category | flops | bytes accessed | tf_op | source)
XLA Modules:
  0.0 534.9 jit_solution(13241130299326977567)
XLA Ops:
  7.9 3.0 collective-permute-start.3
  11.0 24.3 %collective-permute-done.3 = bf16[96,5,768]{2,0,1:T(8,128)(2,1)S(1)} collective-permute-done((bf16[96,5,768]{2,0,1:T(8,128)(2,1)}, bf16[96,5,768]{2,0,1:T(8,128)(2,1)S(1)}, u32[]{:S(2)}, u32[]{:S(2)}) %collective-permute-start.3) | collective-permute-done | bytes 737312 | tf_op jit(solution)/shard_map/ppermute | solution.py:14
  35.7 34.6 %collective-permute-done.4 = bf16[96,5,768]{2,0,1:T(8,128)(2,1)S(1)} collective-permute-done((bf16[96,5,768]{2,0,1:T(8,128)(2,1)S(1)}, bf16[96,5,768]{2,0,1:T(8,128)(2,1)S(1)}, u32[]{:S(2)}, u32[]{:S(2)}) %collective-permute-start.4) | collective-permute-done | bytes 737312 | tf_op jit(solution)/shard_map/ppermute | solution.py:14
  70.3 35.6 %collective-permute-done.5 = bf16[96,5,768]{2,0,1:T(8,128)(2,1)S(1)} collective-permute-done((bf16[96,5,768]{2,0,1:T(8,128)(2,1)S(1)}, bf16[96,5,768]{2,0,1:T(8,128)(2,1)S(1)}, u32[]{:S(2)}, u32[]{:S(2)}) %collective-permute-start.5) | collective-permute-done | bytes 737312 | tf_op jit(solution)/shard_map/ppermute | solution.py:14
  105.9 36.1 %collective-permute-done.6 = bf16[96,5,768]{2,0,1:T(8,128)(2,1)} collective-permute-done((bf16[96,5,768]{2,0,1:T(8,128)(2,1)S(1)}, bf16[96,5,768]{2,0,1:T(8,128)(2,1)}, u32[]{:S(2)}, u32[]{:S(2)}) %collective-permute-start.6) | collective-permute-done | bytes 737312 | tf_op jit(solution)/shard_map/ppermute | solution.py:14
  142.0 2.6 all_gather.7
  145.2 1.3 collective-permute-start.12
  146.5 1.3 collective-permute-start.11
  147.8 2.2 reshape.31
  149.9 1.9 reduce_sum.18
  151.8 17.2 %collective-permute-done.7 = bf16[96,5,768]{2,0,1:T(8,128)(2,1)} collective-permute-done((bf16[96,5,768]{2,0,1:T(8,128)(2,1)}, bf16[96,5,768]{2,0,1:T(8,128)(2,1)}, u32[]{:S(2)}, u32[]{:S(2)}) %collective-permute-start.7) | collective-permute-done | bytes 737312 | tf_op jit(solution)/shard_map/ppermute | solution.py:14
  169.7 1.3 collective-permute-start.1
  171.0 4.5 collective-permute-start
  175.6 2.9 broadcast_in_dim.16
  179.6 7.7 %collective-permute-done.8 = bf16[96,5,768]{2,0,1:T(8,128)(2,1)} collective-permute-done((bf16[96,5,768]{2,0,1:T(8,128)(2,1)}, bf16[96,5,768]{2,0,1:T(8,128)(2,1)}, u32[]{:S(2)}, u32[]{:S(2)}) %collective-permute-start.8) | collective-permute-done | bytes 737312 | tf_op jit(solution)/shard_map/ppermute | solution.py:14
  189.2 2.1 constant_dynamic-update-slice_fusion.6
  191.2 2.1 constant_dynamic-update-slice_fusion.5
  193.3 2.1 constant_dynamic-update-slice_fusion.4
  195.3 2.1 constant_dynamic-update-slice_fusion.3
  197.4 8.2 %collective-permute-done.9 = bf16[96,5,768]{2,0,1:T(8,128)(2,1)S(1)} collective-permute-done((bf16[96,5,768]{2,0,1:T(8,128)(2,1)}, bf16[96,5,768]{2,0,1:T(8,128)(2,1)S(1)}, u32[]{:S(2)}, u32[]{:S(2)}) %collective-permute-start.9) | collective-permute-done | bytes 737312 | tf_op jit(solution)/shard_map/ppermute | solution.py:14
  206.5 2.1 fusion.40
  208.6 2.1 fusion.37
  210.6 2.1 fusion.33
  212.7 2.1 fusion.35
  214.8 3.4 fusion.1
  218.2 2.2 reshape.29
  220.4 1.9 reduce_sum.19
  222.3 1.7 fusion.30
  224.1 1.8 fusion.32
  225.9 1.8 fusion.28
  227.6 1.8 fusion.25
  229.4 2.2 fusion.50
  232.2 1.3 collective-permute-start.10
  233.5 4.5 collective-permute-start.2
  238.8 3.5 fusion.38
  242.9 1.9 collective-permute-start.14
  244.8 1.5 collective-permute-start.13
  247.9 2.7 fusion.29
  250.5 1.2 fusion.19
  251.7 1.2 fusion.21
  252.9 2.5 copy-done
  255.9 1.2 reshape.28
  257.1 3.5 fusion.39
  260.6 3.5 fusion.36
  265.0 3.5 fusion.34
  269.3 4.1 add_convert_fusion
  273.4 1.9 fusion.3
  275.3 1.8 fusion.31
  277.1 1.8 fusion.27
  278.9 1.8 fusion.23
  280.7 2.6 fusion.26
  283.5 3.1 fusion.5
  286.6 1.2 copy.12
  287.8 3.0 fusion.7
  290.9 3.0 fusion.9
  293.9 1.8 fusion.11
  295.7 10.4 %pad_maximum_fusion = bf16[768,5,1536]{0,2,1:T(8,128)(2,1)} fusion(bf16[768,5,768]{0,2,1:T(8,128)(2,1)} %fusion.11, bf16[768,5,768]{0,2,1:T(8,128)(2,1)} %copy-done), kind=kLoop, calls=%fused_computation | loop fusion | flops 23592960 | bytes 23592960 | tf_op jit(solution)/shard_map/concatenate | solution.py:115
  306.1 15.1 %copy.16 = bf16[768,7680]{1,0:T(8,128)(2,1)} copy(bf16[768,7680]{0,1:T(8,128)(2,1)} %bitcast.125) | data formatting | bytes 23592960
  323.9 1.2 copy.13
  326.0 195.1 %reduce-scatter.9.cloned.1.call-done = bf16[96,7680]{1,0:T(8,128)(2,1)} async-done(((bf16[768,7680]{1,0:T(8,128)(2,1)}), bf16[96,7680]{1,0:T(8,128)(2,1)}) %reduce-scatter.9.cloned.1.call-update) | async-done | bytes 1474576
  521.1 2.7 copy.17
  523.9 1.1 fusion.80
  525.0 2.2 copy.10
  527.2 1.2 copy.11
  (78 shorter events, 15.8 us)
Async XLA Ops:
  7.2 215.1 %all-gather.2.cloned.1.call-start = ((), (), s32[]{:S(2)}) async-start(), calls=%async_computation.2 | async-start | bytes 6635520 | tf_op jit(solution)/shard_map/all_gather | solution.py:44
  7.9 313.3 %all-reduce.2.cloned.1.call-start = ((), (), s32[]{:S(2)}) async-start(), calls=%async_computation.3 | async-start | bytes 786432 | tf_op jit(solution)/shard_map/psum | solution.py:95
  7.9 27.3 %collective-permute-start.3 = (bf16[96,5,768]{2,0,1:T(8,128)(2,1)}, bf16[96,5,768]{2,0,1:T(8,128)(2,1)S(1)}, u32[]{:S(2)}, u32[]{:S(2)}) collective-permute-start(bf16[96,5,768]{2,0,1:T(8,128)(2,1)} %param.6), channel_id=1, source_target_pairs={{0,2},{2,4},{4,6},{6,8},{8,10},{10,12},{12,14},{14,0},{1,3},{3,5},... | collective-permute-start | bytes 2211848 | tf_op jit(solution)/shard_map/ppermute | solution.py:14
  35.2 106.8 %copy-start.8 = (bf16[96,5,768]{2,0,1:T(8,128)(2,1)}, bf16[96,5,768]{2,0,1:T(8,128)(2,1)S(1)}, u32[]{:S(2)}) copy-start(bf16[96,5,768]{2,0,1:T(8,128)(2,1)S(1)} %collective-permute-done.3) | copy-start | bytes 2211844
  35.2 35.1 %collective-permute-start.4 = (bf16[96,5,768]{2,0,1:T(8,128)(2,1)S(1)}, bf16[96,5,768]{2,0,1:T(8,128)(2,1)S(1)}, u32[]{:S(2)}, u32[]{:S(2)}) collective-permute-start(bf16[96,5,768]{2,0,1:T(8,128)(2,1)S(1)} %collective-permute-done.3), channel_id=1, source_target_pairs={{0,2},{2,4},{4,6},{6,8},{8,10},{10,12},{12,14},{14,0},{1,3},{3,5},... | collective-permute-start | bytes 2211848 | tf_op jit(solution)/shard_map/ppermute | solution.py:14
  70.3 71.7 %copy-start.10 = (bf16[96,5,768]{2,0,1:T(8,128)(2,1)}, bf16[96,5,768]{2,0,1:T(8,128)(2,1)S(1)}, u32[]{:S(2)}) copy-start(bf16[96,5,768]{2,0,1:T(8,128)(2,1)S(1)} %collective-permute-done.4) | copy-start | bytes 2211844
  70.3 35.6 %collective-permute-start.5 = (bf16[96,5,768]{2,0,1:T(8,128)(2,1)S(1)}, bf16[96,5,768]{2,0,1:T(8,128)(2,1)S(1)}, u32[]{:S(2)}, u32[]{:S(2)}) collective-permute-start(bf16[96,5,768]{2,0,1:T(8,128)(2,1)S(1)} %collective-permute-done.4), channel_id=1, source_target_pairs={{0,2},{2,4},{4,6},{6,8},{8,10},{10,12},{12,14},{14,0},{1,3},{3,5},... | collective-permute-start | bytes 2211848 | tf_op jit(solution)/shard_map/ppermute | solution.py:14
  105.9 36.1 %copy-start.12 = (bf16[96,5,768]{2,0,1:T(8,128)(2,1)}, bf16[96,5,768]{2,0,1:T(8,128)(2,1)S(1)}, u32[]{:S(2)}) copy-start(bf16[96,5,768]{2,0,1:T(8,128)(2,1)S(1)} %collective-permute-done.5) | copy-start | bytes 2211844
  105.9 36.1 %collective-permute-start.6 = (bf16[96,5,768]{2,0,1:T(8,128)(2,1)S(1)}, bf16[96,5,768]{2,0,1:T(8,128)(2,1)}, u32[]{:S(2)}, u32[]{:S(2)}) collective-permute-start(bf16[96,5,768]{2,0,1:T(8,128)(2,1)S(1)} %collective-permute-done.5), channel_id=1, source_target_pairs={{0,2},{2,4},{4,6},{6,8},{8,10},{10,12},{12,14},{14,0},{1,3},{3,5},... | collective-permute-start | bytes 2211848 | tf_op jit(solution)/shard_map/ppermute | solution.py:14
  142.0 27.0 %collective-permute-start.7 = (bf16[96,5,768]{2,0,1:T(8,128)(2,1)}, bf16[96,5,768]{2,0,1:T(8,128)(2,1)}, u32[]{:S(2)}, u32[]{:S(2)}) collective-permute-start(bf16[96,5,768]{2,0,1:T(8,128)(2,1)} %collective-permute-done.6), channel_id=1, source_target_pairs={{0,2},{2,4},{4,6},{6,8},{8,10},{10,12},{12,14},{14,0},{1,3},{3,5},... | collective-permute-start | bytes 2211848 | tf_op jit(solution)/shard_map/ppermute | solution.py:14
  145.2 61.3 %collective-permute-start.12 = (bf16[2,768]{1,0:T(2,128)(2,1)}, bf16[2,768]{1,0:T(2,128)(2,1)S(1)}, u32[]{:S(2)}, u32[]{:S(2)}) collective-permute-start(bf16[2,768]{1,0:T(2,128)(2,1)} %get-tuple-element.17), channel_id=1, source_target_pairs={{0,2},{2,4},{4,6},{6,8},{8,10},{10,12},{12,14},{1,3},{3,5},{5,7},{... | collective-permute-start | bytes 9224 | tf_op jit(solution)/shard_map/ppermute | solution.py:26
  146.5 33.1 %collective-permute-start.11 = (bf16[2,768]{1,0:T(2,128)(2,1)}, bf16[2,768]{1,0:T(2,128)(2,1)S(1)}, u32[]{:S(2)}, u32[]{:S(2)}) collective-permute-start(bf16[2,768]{1,0:T(2,128)(2,1)} %get-tuple-element.16), channel_id=1, source_target_pairs={{2,0},{4,2},{6,4},{8,6},{10,8},{12,10},{14,12},{3,1},{5,3},{7,5},{... | collective-permute-start | bytes 9224 | tf_op jit(solution)/shard_map/ppermute | solution.py:27
  151.8 26.7 %copy-start.7 = (bf16[96,5,768]{2,0,1:T(8,128)(2,1)S(1)}, bf16[96,5,768]{2,0,1:T(8,128)(2,1)}, u32[]{:S(2)}) copy-start(bf16[96,5,768]{2,0,1:T(8,128)(2,1)} %param.6) | copy-start | bytes 2211844
  151.8 35.5 %copy-start.9 = (bf16[96,5,768]{2,0,1:T(8,128)(2,1)S(1)}, bf16[96,5,768]{2,0,1:T(8,128)(2,1)}, u32[]{:S(2)}) copy-start(bf16[96,5,768]{2,0,1:T(8,128)(2,1)} %copy-done.8) | copy-start | bytes 2211844
  169.0 18.3 %collective-permute-start.8 = (bf16[96,5,768]{2,0,1:T(8,128)(2,1)}, bf16[96,5,768]{2,0,1:T(8,128)(2,1)}, u32[]{:S(2)}, u32[]{:S(2)}) collective-permute-start(bf16[96,5,768]{2,0,1:T(8,128)(2,1)} %collective-permute-done.7), channel_id=1, source_target_pairs={{0,2},{2,4},{4,6},{6,8},{8,10},{10,12},{12,14},{14,0},{1,3},{3,5},... | collective-permute-start | bytes 2211848 | tf_op jit(solution)/shard_map/ppermute | solution.py:14
  169.1 19.2 %copy-start.11 = (bf16[96,5,768]{2,0,1:T(8,128)(2,1)S(1)}, bf16[96,5,768]{2,0,1:T(8,128)(2,1)}, u32[]{:S(2)}) copy-start(bf16[96,5,768]{2,0,1:T(8,128)(2,1)} %copy-done.10) | copy-start | bytes 2211844
  169.7 54.4 %collective-permute-start.1 = (bf16[2,768]{1,0:T(2,128)(2,1)}, bf16[2,768]{1,0:T(2,128)(2,1)}, u32[]{:S(2)}, u32[]{:S(2)}) collective-permute-start(bf16[2,768]{1,0:T(2,128)(2,1)} %get-tuple-element.25), channel_id=1, source_target_pairs={{2,0},{4,2},{6,4},{8,6},{10,8},{12,10},{14,12},{3,1},{5,3},{7,5},{... | collective-permute-start | bytes 9224 | tf_op jit(solution)/shard_map/ppermute | solution.py:27
  171.0 54.9 %collective-permute-start = (bf16[2,768]{1,0:T(2,128)(2,1)S(1)}, bf16[2,768]{1,0:T(2,128)(2,1)S(1)}, u32[]{:S(2)}, u32[]{:S(2)}) collective-permute-start(bf16[2,768]{1,0:T(2,128)(2,1)S(1)} %get-tuple-element.24), channel_id=1, source_target_pairs={{0,2},{2,4},{4,6},{6,8},{8,10},{10,12},{12,14},{1,3},{3,5},{5,7},{... | collective-permute-start | bytes 9224 | tf_op jit(solution)/shard_map/ppermute | solution.py:26
  187.3 18.3 %collective-permute-start.9 = (bf16[96,5,768]{2,0,1:T(8,128)(2,1)}, bf16[96,5,768]{2,0,1:T(8,128)(2,1)S(1)}, u32[]{:S(2)}, u32[]{:S(2)}) collective-permute-start(bf16[96,5,768]{2,0,1:T(8,128)(2,1)} %collective-permute-done.8), channel_id=1, source_target_pairs={{0,2},{2,4},{4,6},{6,8},{8,10},{10,12},{12,14},{14,0},{1,3},{3,5},... | collective-permute-start | bytes 2211848 | tf_op jit(solution)/shard_map/ppermute | solution.py:14
  232.2 23.2 %collective-permute-start.10 = (bf16[1,768]{1,0:T(2,128)(2,1)}, bf16[1,768]{1,0:T(2,128)(2,1)S(1)}, u32[]{:S(2)}, u32[]{:S(2)}) collective-permute-start(bf16[1,768]{1,0:T(2,128)(2,1)} %get-tuple-element.23), channel_id=1, source_target_pairs={{2,0},{4,2},{6,4},{8,6},{10,8},{12,10},{14,12},{3,1},{5,3},{7,5},{... | collective-permute-start | bytes 4616 | tf_op jit(solution)/shard_map/ppermute | solution.py:27
  233.5 21.9 %collective-permute-start.2 = (bf16[1,768]{1,0:T(2,128)(2,1)}, bf16[1,768]{1,0:T(2,128)(2,1)S(1)}, u32[]{:S(2)}, u32[]{:S(2)}) collective-permute-start(bf16[1,768]{1,0:T(2,128)(2,1)} %get-tuple-element.22), channel_id=1, source_target_pairs={{0,2},{2,4},{4,6},{6,8},{8,10},{10,12},{12,14},{1,3},{3,5},{5,7},{... | collective-permute-start | bytes 4616 | tf_op jit(solution)/shard_map/ppermute | solution.py:26
  238.8 11.8 %copy-start.4 = (bf16[512,768]{1,0:T(8,128)(2,1)}, bf16[512,768]{1,0:T(8,128)(2,1)S(1)}, u32[]{:S(2)}) copy-start(bf16[512,768]{1,0:T(8,128)(2,1)S(1)} %slice.174) | copy-start | bytes 2359300
  242.9 32.4 %collective-permute-start.14 = (bf16[2,768]{1,0:T(2,128)(2,1)}, bf16[2,768]{1,0:T(2,128)(2,1)S(1)}, u32[]{:S(2)}, u32[]{:S(2)}) collective-permute-start(bf16[2,768]{1,0:T(2,128)(2,1)} %get-tuple-element.19), channel_id=1, source_target_pairs={{0,2},{2,4},{4,6},{6,8},{8,10},{10,12},{12,14},{1,3},{3,5},{5,7},{... | collective-permute-start | bytes 9224 | tf_op jit(solution)/shard_map/ppermute | solution.py:26
  244.8 32.3 %collective-permute-start.13 = (bf16[2,768]{1,0:T(2,128)(2,1)}, bf16[2,768]{1,0:T(2,128)(2,1)}, u32[]{:S(2)}, u32[]{:S(2)}) collective-permute-start(bf16[2,768]{1,0:T(2,128)(2,1)} %get-tuple-element.18), channel_id=1, source_target_pairs={{2,0},{4,2},{6,4},{8,6},{10,8},{12,10},{14,12},{3,1},{5,3},{7,5},{... | collective-permute-start | bytes 9224 | tf_op jit(solution)/shard_map/ppermute | solution.py:27
  252.9 2.5 copy-start
  265.0 3.5 copy-start.5
  269.3 4.1 copy-start.6
  273.4 5.5 %copy-start.1 = (f32[256,768]{1,0:T(8,128)S(1)}, f32[256,768]{1,0:T(8,128)}, u32[]{:S(2)}) copy-start(f32[256,768]{1,0:T(8,128)} %fusion.29) | copy-start | bytes 2359300
  283.2 40.7 %reduce-scatter.7.cloned.1.call-start = ((), (), s32[]{:S(2)}) async-start(), calls=%async_computation.4 | async-start | bytes 1179648
  290.8 230.3 %reduce-scatter.9.cloned.1.call-start = ((), (), s32[]{:S(2)}) async-start(), calls=%async_computation.5 | async-start | bytes 13271040
  321.2 1.9 copy-start.3
  321.2 4.0 copy-start.2
Sparse Core Ops, SparseCore 0:
  10.2 142.0 all-gather.1
  283.4 22.0 all-reduce.1
  307.8 9.4 reduce-scatter.6
  321.3 199.7 reduce-scatter.8
